TPU v7x, 32 devices: a whole 2x2x4 slice. The times are simulated.
32 devices in a mesh: tm: 4 (over y, x), space: 8 (over z, core).
Axes of the slice: x: 2, y: 2, z: 4, core: 2. Of those that a mesh axis runs over, the one named last changes fastest.
Arguments:
- frames_in: bfloat16 [32, 512, 1024], P('tm', 'space'), may hold values from -6 to 6
- time_gain: float32 [1024], replicated, may hold values from 0.1 to 1.9
- time_shift: float32 [1024], replicated, may hold values from -4 to 4
- time_query: bfloat16 [1024, 1024], replicated
- time_key: bfloat16 [1024, 1024], replicated
- time_value: bfloat16 [1024, 1024], replicated, may hold values from -0.1875 to 0.1875
- time_out: bfloat16 [1024, 1024], replicated, may hold values from -0.1875 to 0.1875
- space_gain: float32 [1024], replicated, may hold values from 0.1 to 1.9
- space_shift: float32 [1024], replicated, may hold values from -4 to 4
- space_query: bfloat16 [1024, 1024], replicated
- space_key: bfloat16 [1024, 1024], replicated
- space_value: bfloat16 [1024, 1024], replicated, may hold values from -0.1875 to 0.1875
- space_out: bfloat16 [1024, 1024], replicated, may hold values from -0.1875 to 0.1875
Outputs:
- frames_out: bfloat16 [32, 512, 1024], P('tm', 'space')
All inputs are finite; a program needn't handle non-finite values.
Results may differ from a plain program's by a relative error of at most 0.03.
Values may be sent and summed in bfloat16 or wider, within the bound.
A program may use at most 192 MiB of HBM per device.

v0:
```python
import functools
import math

import jax
import jax.numpy as jnp
from jax import lax
from jax.experimental import pallas as pl
from jax.experimental.pallas import tpu as pltpu
from jax.sharding import PartitionSpec as P

HEAD_DIM = 64
LANES = 128
SCALE = 0.125 * math.log2(math.e)
F32, BF16 = jnp.float32, jnp.bfloat16


def layer_norm(tokens, gain, shift):
    values = tokens.astype(F32)
    mean_value = jnp.mean(values, axis=-1, keepdims=True)
    centred = values - mean_value
    variance = jnp.mean(centred * centred, axis=-1, keepdims=True)
    return (centred * lax.rsqrt(variance + 1e-05) * gain + shift).astype(BF16)


def project(tokens, weight):
    return jnp.dot(tokens, weight, preferred_element_type=F32)


def permutation(rows, inner, outer, back):
    row = lax.broadcasted_iota(jnp.int32, (rows, rows), 1 if back else 0)
    col = lax.broadcasted_iota(jnp.int32, (rows, rows), 0 if back else 1)
    return jnp.where((row % inner) * outer + row // inner == col, 1.0, 0.0).astype(BF16)


def lane_masks(width):
    lane = lax.broadcasted_iota(jnp.int32, (1, LANES), 1)
    return [(lane // HEAD_DIM == part) for part in range(LANES // HEAD_DIM)]


def attend(queries, keys_in, values_in, same):
    rows = queries.shape[0]
    masks = lane_masks(LANES)
    own = jnp.concatenate([jnp.where(mask, queries, jnp.zeros_like(queries)) for mask in masks], 0)
    scores = lax.dot_general(own, keys_in, (((1,), (1,)), ((), ())), preferred_element_type=F32)
    if same is not None:
        scores = jnp.where(jnp.concatenate([same] * len(masks), 0), scores, -1e30)
    top = jnp.max(scores, axis=-1, keepdims=True)
    weights = jnp.exp2((scores - top) * SCALE).astype(BF16)
    both = jnp.concatenate([values_in, jnp.ones_like(values_in)], 1)
    added = jnp.dot(weights, both, preferred_element_type=F32)
    added = added[:, :LANES] / added[:, LANES:]
    result = added[:rows]
    for part in range(1, len(masks)):
        result = jnp.where(masks[part], added[part * rows : (part + 1) * rows], result)
    return result.astype(BF16)


def qkv(normed, weights, waits, outs):
    for weight, wait, out in zip(weights, waits, outs):
        wait()
        out[...] = project(normed, weight[...]).astype(BF16)


def time_branch(frames, x, gain, shift, weights, waits, q, k, v, a):
    rows, width = q.shape
    places = rows // frames
    order = permutation(rows, frames, places, False)
    x = project(order, x).astype(BF16)
    qkv(layer_norm(x, gain, shift), weights[:3], waits[:3], (q, k, v))
    size = max(frames, LANES)
    same = (
        lax.broadcasted_iota(jnp.int32, (size, size), 0) // frames
        == lax.broadcasted_iota(jnp.int32, (size, size), 1) // frames
    )

    def pair(index, carry):
        cols = pl.ds(pl.multiple_of(index * LANES, LANES), LANES)
        for group in range(rows // size):
            part = (pl.ds(group * size, size), cols)
            a[part] = attend(q[part], k[part], v[part], same)
        return carry

    lax.fori_loop(0, width // LANES, pair, 0, unroll=2)
    waits[3]()
    after = (x.astype(F32) + project(a[...], weights[3][...])).astype(BF16)
    return project(permutation(rows, frames, places, True), after)


def branch_kernel(branch, x, gain, shift, w0, w1, w2, w3, out, held, q, k, v, a, sems):
    copies = [
        pltpu.make_async_copy(w, held.at[i], sems.at[i]) for i, w in enumerate((w0, w1, w2, w3))
    ]
    for copy in copies:
        copy.start()
    weights = [held.at[i] for i in range(4)]
    waits = [copy.wait for copy in copies]
    out[...] = branch(x[...], gain[...], shift[...], weights, waits, q, k, v, a).astype(BF16)


def run_branch(branch, x, gain, shift, *weights):
    rows, width = x.shape
    vmem = pl.BlockSpec(memory_space=pltpu.VMEM)
    return pl.pallas_call(
        functools.partial(branch_kernel, branch),
        out_shape=jax.ShapeDtypeStruct((rows, width), BF16),
        in_specs=[vmem] * 3 + [pl.BlockSpec(memory_space=pl.ANY)] * 4,
        out_specs=vmem,
        scratch_shapes=[pltpu.VMEM((4, width, width), BF16)]
        + [pltpu.VMEM((rows, width), BF16)] * 4
        + [pltpu.SemaphoreType.DMA((4,))],
        compiler_params=pltpu.CompilerParams(vmem_limit_bytes=60 << 20),
    )(x, gain.reshape(1, -1), shift.reshape(1, -1), *weights)


def flipped(index, mask):
    result, bit = index + mask, 1
    while bit < 64:
        result = result - 2 * bit * ((index // bit) % 2) * ((mask // bit) % 2)
        bit *= 2
    return result


def layer_kernel(
    slots,
    spread,
    x,
    tg,
    ts,
    sg,
    ss,
    *refs,
):
    sources, out = refs[:8], refs[8]
    held, xt, snd, rcv, q, k, v, a, wsem, lsem, s1, r1, s2, r2, s3, r3 = refs[9:]
    me_t, me_s = lax.axis_index("tm"), lax.axis_index("space")
    frames, piece, width = xt.shape[1:]
    rows, halves = frames // slots, xt.shape[0]
    peers = slots * spread
    tokens = frames * piece

    def device(mask):
        return flipped(me_t, mask % slots), flipped(me_s, mask // slots)

    barrier = pltpu.get_barrier_semaphore()

    def greet(n, carry):
        t, s = device(n + 1)
        pl.semaphore_signal(barrier, inc=1, device_id={"tm": t, "space": s})
        return carry

    lax.fori_loop(0, peers - 1, greet, 0)
    loads = [pltpu.make_async_copy(w, held.at[i], wsem.at[i]) for i, w in enumerate(sources)]
    locals_in = [
        pltpu.make_async_copy(
            x.at[:, me_t, h], xt.at[h, pl.ds(me_t * rows, rows)], lsem.at[h]
        )
        for h in range(halves)
    ]
    for copy in locals_in + loads:
        copy.start()
    pl.semaphore_wait(barrier, peers - 1)

    def first(h, mask):
        t = flipped(me_t, mask)
        return pltpu.make_async_remote_copy(
            src_ref=x.at[:, t, h],
            dst_ref=xt.at[h, pl.ds(me_t * rows, rows)],
            send_sem=s1.at[h, mask],
            recv_sem=r1.at[h, mask],
            device_id={"tm": t},
        )

    def second(h, mask):
        t, s = device(mask)
        return pltpu.make_async_remote_copy(
            src_ref=snd.at[h, t * rows + s],
            dst_ref=rcv.at[h * peers + me_s * slots + me_t],
            send_sem=s2.at[h, mask],
            recv_sem=r2.at[h, mask],
            device_id={"tm": t, "space": s},
        )

    for h in range(halves):
        for mask in range(slots - 1, 0, -1):
            first(h, mask).start()

    weights = [held.at[i] for i in range(8)]
    waits = [copy.wait for copy in loads]
    for h in range(halves):
        locals_in[h].wait()
        for mask in range(1, slots):
            first(h, mask).wait_recv()
        part = [ref.at[pl.ds(0, tokens)] for ref in (q, k, v, a)]
        after = time_branch(
            frames,
            xt[h].astype(F32).reshape(tokens, width).astype(BF16),
            tg[...],
            ts[...],
            weights[:4],
            waits[:4] if h == 0 else [lambda: None] * 4,
            *part,
        )
        after = after.reshape(frames, piece, width).astype(BF16)
        snd[h] = after

        def send(n, carry):
            second(h, peers - 1 - n).start()
            return carry

        lax.fori_loop(0, peers - 1, send, 0)
        rcv[h * peers + me_s * slots + me_t] = snd[h, me_t * rows + me_s]

    for h in range(halves):

        def arrive(n, carry):
            second(h, peers - 1 - n).wait_recv()
            return carry

        lax.fori_loop(0, peers - 1, arrive, 0)
        frame = rcv[pl.ds(h * peers, peers)].astype(F32).reshape(tokens, width).astype(BF16)
        qkv(
            layer_norm(frame, sg[...], ss[...]),
            weights[4:7],
            waits[4:7] if h == 0 else [lambda: None] * 3,
            [ref.at[pl.ds(h * tokens, tokens)] for ref in (q, k, v)],
        )
    waits[7]()
    share = slots * piece
    group = 2 if spread % 2 == 0 else 1
    steps = spread // group

    def blocks(h, s, count):
        return pl.ds(h * peers + s * slots, count * slots)

    def third(h, mask):
        s = flipped(me_s, mask)
        return pltpu.make_async_remote_copy(
            src_ref=rcv.at[blocks(h, s, 1)],
            dst_ref=out.at[me_s, :, h],
            send_sem=s3.at[h, mask],
            recv_sem=r3.at[h, mask],
            device_id={"space": s},
        )

    for step in range(steps - 1, -1, -1):
        size = group * share
        base = flipped(me_s // group, step) * group
        parts = [
            pl.ds(pl.multiple_of(h * tokens + base * share, size), size) for h in range(halves)
        ]

        def pair(index, carry):
            cols = pl.ds(pl.multiple_of(index * LANES, LANES), LANES)
            queries = jnp.concatenate([q[part, cols] for part in parts], 0)
            result = attend(queries, k[:, cols], v[:, cols], None)
            for h, part in enumerate(parts):
                a[part, cols] = result[h * size : (h + 1) * size]
            return carry

        lax.fori_loop(0, width // LANES, pair, 0, unroll=2)
        added = project(jnp.concatenate([a[part] for part in parts], 0), weights[7][...])
        for h in range(halves):
            here = blocks(h, base, group)
            new = added[h * size : (h + 1) * size].reshape(group * slots, piece, width)
            rcv[here] = (rcv[here].astype(F32) + new).astype(BF16)
        for member in range(group - 1, -1, -1):
            if step * group + member:
                for h in range(halves):
                    third(h, step * group + member).start()
    last = [
        pltpu.make_async_copy(rcv.at[blocks(h, me_s, 1)], out.at[me_s, :, h], lsem.at[h])
        for h in range(halves)
    ]
    for copy in last:
        copy.start()
    for h in range(halves):
        for mask in range(1, slots):
            first(h, mask).wait_send()

    def left(n, carry):
        for h in range(halves):
            second(h, n + 1).wait_send()
        return carry

    lax.fori_loop(0, peers - 1, left, 0)
    for h in range(halves):
        for mask in range(1, spread):
            third(h, mask).wait()
        last[h].wait()


def run_layer(frames_in, slots, spread, norms, weights):
    rows, patches, width = frames_in.shape
    frames, places, halves = rows * slots, patches // slots, 2
    piece = places // halves
    total = frames * places
    vmem, hbm = pl.BlockSpec(memory_space=pltpu.VMEM), pl.BlockSpec(memory_space=pltpu.HBM)
    dma = pltpu.SemaphoreType.DMA
    return pl.pallas_call(
        functools.partial(layer_kernel, slots, spread),
        out_shape=jax.ShapeDtypeStruct((rows, slots, halves, piece, width), BF16),
        in_specs=[hbm] + [vmem] * 4 + [hbm] * 8,
        out_specs=hbm,
        scratch_shapes=[
            pltpu.VMEM((8, width, width), BF16),
            pltpu.VMEM((halves, frames, piece, width), BF16),
            pltpu.VMEM((halves, frames, piece, width), BF16),
            pltpu.VMEM((total // piece, piece, width), BF16),
        ]
        + [pltpu.VMEM((total, width), BF16)] * 4
        + [
            dma((8,)),
            dma((halves,)),
            dma((halves, slots)),
            dma((halves, slots)),
            dma((halves, slots * spread)),
            dma((halves, slots * spread)),
            dma((halves, spread)),
            dma((halves, spread)),
        ],
        compiler_params=pltpu.CompilerParams(
            collective_id=0, has_side_effects=True, vmem_limit_bytes=60 << 20
        ),
    )(
        frames_in.reshape(rows, slots, halves, piece, width),
        *[norm.reshape(1, -1) for norm in norms],
        *weights,
    ).reshape(frames_in.shape)


def split_heads(tokens):
    return tokens.reshape(tokens.shape[0], tokens.shape[1], tokens.shape[2] // HEAD_DIM, HEAD_DIM)


def gathered_space(after_time, gain, shift, wq, wk, wv, wo):
    normed = layer_norm(after_time, gain, shift)
    queries = project(normed, wq).astype(BF16)
    everywhere = lax.all_gather(normed, "space", axis=1, tiled=True)
    keys_in, values_in = (project(everywhere, w).astype(BF16) for w in (wk, wv))
    scores = 0.125 * jnp.einsum(
        "fqhd,fkhd->fhqk", split_heads(queries), split_heads(keys_in), preferred_element_type=F32
    )
    weights = jax.nn.softmax(scores, axis=-1).astype(BF16)
    spatial = jnp.einsum(
        "fhqk,fkhd->fqhd", weights, split_heads(values_in), preferred_element_type=F32
    )
    spatial = spatial.astype(BF16).reshape(after_time.shape)
    return (after_time.astype(F32) + project(spatial, wo)).astype(BF16)


def body(frames_in, tg, ts, tq, tk, tv, to, sg, ss, sq, sk, sv, so):
    slots, spread = lax.axis_size("tm"), lax.axis_size("space")
    rows, patches, width = frames_in.shape
    frames, places = rows * slots, patches // slots
    if rows == spread and not (slots & (slots - 1) or spread & (spread - 1)):
        return run_layer(
            frames_in, slots, spread, (tg, ts, sg, ss), (tq, tk, tv, to, sq, sk, sv, so)
        )
    tokens = lax.all_to_all(
        frames_in.reshape(rows, slots, places, width), "tm", split_axis=1, concat_axis=0, tiled=True
    ).reshape(frames * places, width)
    after = run_branch(functools.partial(time_branch, frames), tokens, tg, ts, tq, tk, tv, to)
    after = lax.all_to_all(
        after.reshape(frames, 1, places, width), "tm", split_axis=0, concat_axis=1, tiled=True
    ).reshape(rows, patches, width)
    return gathered_space(after, sg, ss, sq, sk, sv, so)


def solution(mesh):
    return jax.shard_map(
        body,
        mesh=mesh,
        in_specs=(P("tm", "space", None),) + (P(),) * 12,
        out_specs=P("tm", "space", None),
        check_vma=False,
    )
```

profile of v0, /device:TPU:0, one launch (start us, length us, event | category | flops | bytes accessed | tf_op | source)
XLA Modules:
  0.0 80.3 jit_solution(13955742200642388116)
XLA Ops:
  0.0 78.0 %shard_map.127 = bf16[8,4,2,8,1024]{4,3,2,1,0:T(8,128)(2,1)} custom-call(bf16[8,4,2,8,1024]{4,3,2,1,0:T(8,128)(2,1)} %bitcast.7, f32[1,1024]{1,0:T(1,128)} %bitcast.8, f32[1,1024]{1,0:T(1,128)} %bitcast.9, f32[1,1024]{1,0:T(1,128)} %bitcast.10, f32[1,1024]{1,0:T(1,128)} %bitcast.11, bf16[1024,1024]{1,0:T(8,128)(2,1)} %refs_0_.1, bf16[1024,1024]{1,0:T(8,128)(2,1)} %refs_1_.1, ...), custom_call_target="tpu_custom_call" | custom-call | tf_op jit(solution)/shard_map/pallas_call | solution.py:299
  78.0 2.3 %copy.15 = bf16[8,64,1024]{2,1,0:T(8,128)(2,1)} copy(bf16[8,64,1024]{2,1,0:T(8,128)(2,1)} %bitcast.6) | data formatting | bytes 2097152
where the time goes:
time: 80.5 us; the launch traced here: 80.3 us
  Pallas kernels  78 us (97%)
  local copies, waits for them, and re-layouts  2.26 us (3%)
    pallas_call x1, Pallas kernels, run_layer(): pl.pallas_call(functools.partial(layer_kernel, slots, spread), out_shape=...  78 us
    unnamed x1, local copies, waits for them, and re-layouts  2.26 us

commit v1 on v0

--- a/solution.py
+++ b/solution.py
@@ -10,6 +10,7 @@
 
 HEAD_DIM = 64
 LANES = 128
+UNROLL_T, UNROLL_S = 8, 8
 SCALE = 0.125 * math.log2(math.e)
 F32, BF16 = jnp.float32, jnp.bfloat16
 
@@ -80,7 +81,7 @@
             a[part] = attend(q[part], k[part], v[part], same)
         return carry
 
-    lax.fori_loop(0, width // LANES, pair, 0, unroll=2)
+    lax.fori_loop(0, width // LANES, pair, 0, unroll=UNROLL_T)
     waits[3]()
     after = (x.astype(F32) + project(a[...], weights[3][...])).astype(BF16)
     return project(permutation(rows, frames, places, True), after)
@@ -112,12 +113,19 @@
     )(x, gain.reshape(1, -1), shift.reshape(1, -1), *weights)
 
 
-def flipped(index, mask):
-    result, bit = index + mask, 1
-    while bit < 64:
-        result = result - 2 * bit * ((index // bit) % 2) * ((mask // bit) % 2)
+def bit_steps(index, count):
+    out, bit = [], 1
+    while bit < count:
+        out.append((bit, bit - 2 * bit * ((index // bit) % 2)))
         bit *= 2
-    return result
+    return out
+
+
+def moved(index, steps, mask):
+    for bit, step in steps:
+        if mask & bit:
+            index = index + step
+    return index
 
 
 def layer_kernel(
@@ -136,19 +144,23 @@
     frames, piece, width = xt.shape[1:]
     rows, halves = frames // slots, xt.shape[0]
     peers = slots * spread
+    chips = spread // 2
     tokens = frames * piece
-
-    def device(mask):
-        return flipped(me_t, mask % slots), flipped(me_s, mask // slots)
+    me_c = me_s % 2
+    me_z = me_s // 2
+    steps_t, steps_s = bit_steps(me_t, slots), bit_steps(me_s, spread)
+    steps_z = bit_steps(me_z, chips)
 
     barrier = pltpu.get_barrier_semaphore()
-
-    def greet(n, carry):
-        t, s = device(n + 1)
-        pl.semaphore_signal(barrier, inc=1, device_id={"tm": t, "space": s})
-        return carry
-
-    lax.fori_loop(0, peers - 1, greet, 0)
+    for mask in range(1, peers):
+        pl.semaphore_signal(
+            barrier,
+            inc=1,
+            device_id={
+                "tm": moved(me_t, steps_t, mask % slots),
+                "space": moved(me_s, steps_s, mask // slots),
+            },
+        )
     loads = [pltpu.make_async_copy(w, held.at[i], wsem.at[i]) for i, w in enumerate(sources)]
     locals_in = [
         pltpu.make_async_copy(
@@ -161,7 +173,7 @@
     pl.semaphore_wait(barrier, peers - 1)
 
     def first(h, mask):
-        t = flipped(me_t, mask)
+        t = moved(me_t, steps_t, mask)
         return pltpu.make_async_remote_copy(
             src_ref=x.at[:, t, h],
             dst_ref=xt.at[h, pl.ds(me_t * rows, rows)],
@@ -170,14 +182,23 @@
             device_id={"tm": t},
         )
 
-    def second(h, mask):
-        t, s = device(mask)
+    def second(h, mask, core):
+        t, z = moved(me_t, steps_t, mask % slots), moved(me_z, steps_z, mask // slots)
         return pltpu.make_async_remote_copy(
-            src_ref=snd.at[h, t * rows + s],
+            src_ref=snd.at[h, (t * chips + z) * 2 + core],
             dst_ref=rcv.at[h * peers + me_s * slots + me_t],
-            send_sem=s2.at[h, mask],
-            recv_sem=r2.at[h, mask],
-            device_id={"tm": t, "space": s},
+            send_sem=s2.at[h, mask, core],
+            recv_sem=r2.at[h, mask, me_c],
+            device_id={"tm": t, "space": z * 2 + core},
+        )
+
+    def second_wait(h, mask, core):
+        return pltpu.make_async_remote_copy(
+            src_ref=snd.at[0, 0],
+            dst_ref=rcv.at[0],
+            send_sem=s2.at[h, mask, core],
+            recv_sem=r2.at[h, mask, core],
+            device_id={"tm": me_t, "space": me_s + 1 - 2 * me_c},
         )
 
     for h in range(halves):
@@ -186,6 +207,13 @@
 
     weights = [held.at[i] for i in range(8)]
     waits = [copy.wait for copy in loads]
+
+    def send(h, core, masks):
+        for mask in masks:
+            second(h, mask, core).start()
+
+    everyone = list(range(slots * chips - 1, 0, -1))
+    late = []
     for h in range(halves):
         locals_in[h].wait()
         for mask in range(1, slots):
@@ -200,23 +228,28 @@
             waits[:4] if h == 0 else [lambda: None] * 4,
             *part,
         )
-        after = after.reshape(frames, piece, width).astype(BF16)
-        snd[h] = after
-
-        def send(n, carry):
-            second(h, peers - 1 - n).start()
-            return carry
-
-        lax.fori_loop(0, peers - 1, send, 0)
+        snd[h] = after.reshape(frames, piece, width).astype(BF16)
+        send(h, 0, everyone)
+        if h < halves - 1:
+            late.append(h)
+        else:
+            for held_back in late + [h]:
+                send(held_back, 1, everyone)
+        other = 1 - me_c
+        pltpu.make_async_remote_copy(
+            src_ref=snd.at[h, (me_t * chips + me_z) * 2 + other],
+            dst_ref=rcv.at[h * peers + me_s * slots + me_t],
+            send_sem=s2.at[h, 0, 0],
+            recv_sem=r2.at[h, 0, 0],
+            device_id={"space": me_z * 2 + other},
+        ).start()
         rcv[h * peers + me_s * slots + me_t] = snd[h, me_t * rows + me_s]
 
     for h in range(halves):
-
-        def arrive(n, carry):
-            second(h, peers - 1 - n).wait_recv()
-            return carry
-
-        lax.fori_loop(0, peers - 1, arrive, 0)
+        for mask in everyone:
+            for core in range(2):
+                second_wait(h, mask, core).wait_recv()
+        second_wait(h, 0, 0).wait_recv()
         frame = rcv[pl.ds(h * peers, peers)].astype(F32).reshape(tokens, width).astype(BF16)
         qkv(
             layer_norm(frame, sg[...], ss[...]),
@@ -233,7 +266,7 @@
         return pl.ds(h * peers + s * slots, count * slots)
 
     def third(h, mask):
-        s = flipped(me_s, mask)
+        s = moved(me_s, steps_s, mask)
         return pltpu.make_async_remote_copy(
             src_ref=rcv.at[blocks(h, s, 1)],
             dst_ref=out.at[me_s, :, h],
@@ -244,12 +277,12 @@
 
     for step in range(steps - 1, -1, -1):
         size = group * share
-        base = flipped(me_s // group, step) * group
+        base = moved(me_s // group, bit_steps(me_s // group, steps), step) * group
         parts = [
             pl.ds(pl.multiple_of(h * tokens + base * share, size), size) for h in range(halves)
         ]
 
-        def pair(index, carry):
+        def attend_pair(index, carry):
             cols = pl.ds(pl.multiple_of(index * LANES, LANES), LANES)
             queries = jnp.concatenate([q[part, cols] for part in parts], 0)
             result = attend(queries, k[:, cols], v[:, cols], None)
@@ -257,7 +290,7 @@
                 a[part, cols] = result[h * size : (h + 1) * size]
             return carry
 
-        lax.fori_loop(0, width // LANES, pair, 0, unroll=2)
+        lax.fori_loop(0, width // LANES, attend_pair, 0, unroll=UNROLL_S)
         added = project(jnp.concatenate([a[part] for part in parts], 0), weights[7][...])
         for h in range(halves):
             here = blocks(h, base, group)
@@ -277,12 +310,11 @@
         for mask in range(1, slots):
             first(h, mask).wait_send()
 
-    def left(n, carry):
-        for h in range(halves):
-            second(h, n + 1).wait_send()
-        return carry
-
-    lax.fori_loop(0, peers - 1, left, 0)
+    for h in range(halves):
+        for mask in everyone:
+            for core in range(2):
+                second_wait(h, mask, core).wait_send()
+        second_wait(h, 0, 0).wait_send()
     for h in range(halves):
         for mask in range(1, spread):
             third(h, mask).wait()
@@ -313,8 +345,8 @@
             dma((halves,)),
             dma((halves, slots)),
             dma((halves, slots)),
-            dma((halves, slots * spread)),
-            dma((halves, slots * spread)),
+            dma((halves, slots * spread // 2, 2)),
+            dma((halves, slots * spread // 2, 2)),
             dma((halves, spread)),
             dma((halves, spread)),
         ],
@@ -352,7 +384,7 @@
     slots, spread = lax.axis_size("tm"), lax.axis_size("space")
     rows, patches, width = frames_in.shape
     frames, places = rows * slots, patches // slots
-    if rows == spread and not (slots & (slots - 1) or spread & (spread - 1)):
+    if rows == spread and spread % 2 == 0 and not (slots & (slots - 1) or spread & (spread - 1)):
         return run_layer(
             frames_in, slots, spread, (tg, ts, sg, ss), (tq, tk, tv, to, sq, sk, sv, so)
         )

time: 80.5 us -> 71.6 us (0.89)
  Pallas kernels: 78 us -> 68.3 us
    pallas_call x1, Pallas kernels: 78 us -> 68.3 us  [run_layer(): pl.pallas_call(functools.partial(layer_kernel, slots, spread), out_shape=...]
where the time goes in v1:
time: 71.6 us; the launch traced here: 70.6 us
  Pallas kernels  68.3 us (95%)
  local copies, waits for them, and re-layouts  2.26 us (3%)
    pallas_call x1, Pallas kernels, run_layer(): pl.pallas_call(functools.partial(layer_kernel, slots, spread), out_shape=...  68.3 us
    unnamed x1, local copies, waits for them, and re-layouts  2.26 us

profile of v1, /device:TPU:0, one launch (start us, length us, event | category | flops | bytes accessed | tf_op | source)
XLA Modules:
  0.0 70.6 jit_solution(6526856915815895250)
XLA Ops:
  0.0 68.3 %shard_map.127 = bf16[8,4,2,8,1024]{4,3,2,1,0:T(8,128)(2,1)} custom-call(bf16[8,4,2,8,1024]{4,3,2,1,0:T(8,128)(2,1)} %bitcast.7, f32[1,1024]{1,0:T(1,128)} %bitcast.8, f32[1,1024]{1,0:T(1,128)} %bitcast.9, f32[1,1024]{1,0:T(1,128)} %bitcast.10, f32[1,1024]{1,0:T(1,128)} %bitcast.11, bf16[1024,1024]{1,0:T(8,128)(2,1)} %refs_0_.1, bf16[1024,1024]{1,0:T(8,128)(2,1)} %refs_1_.1, ...), custom_call_target="tpu_custom_call" | custom-call | tf_op jit(solution)/shard_map/pallas_call | solution.py:331
  68.4 2.3 %copy.15 = bf16[8,64,1024]{2,1,0:T(8,128)(2,1)} copy(bf16[8,64,1024]{2,1,0:T(8,128)(2,1)} %bitcast.6) | data formatting | bytes 2097152

commit v2 on v1

--- a/solution.py
+++ b/solution.py
@@ -128,6 +128,16 @@
     return index
 
 
+def one_hot(shape, source):
+    row = lax.broadcasted_iota(jnp.int32, shape, 0)
+    col = lax.broadcasted_iota(jnp.int32, shape, 1)
+    return jnp.where(source(row) == col, 1.0, 0.0).astype(BF16)
+
+
+def flat(block):
+    return block.astype(F32).reshape(-1, block.shape[-1]).astype(BF16)
+
+
 def layer_kernel(
     slots,
     spread,
@@ -139,10 +149,13 @@
     *refs,
 ):
     sources, out = refs[:8], refs[8]
-    held, xt, snd, rcv, q, k, v, a, wsem, lsem, s1, r1, s2, r2, s3, r3 = refs[9:]
+    held, xv, xs, xt, snd, rcv, res, q, k, v, a, wsem, lsem, s1, r1, s2, r2, s3, r3 = refs[9:]
     me_t, me_s = lax.axis_index("tm"), lax.axis_index("space")
-    frames, piece, width = xt.shape[1:]
-    rows, halves = frames // slots, xt.shape[0]
+    halves, rows, _, piece, width = xv.shape
+    chunks, size, _ = xt.shape
+    frames = rows * slots
+    few = size // frames
+    fold = piece // few
     peers = slots * spread
     chips = spread // 2
     tokens = frames * piece
@@ -151,6 +164,9 @@
     steps_t, steps_s = bit_steps(me_t, slots), bit_steps(me_s, spread)
     steps_z = bit_steps(me_z, chips)
 
+    halves_in = [pltpu.make_async_copy(x.at[:, :, h], xv.at[h], lsem.at[h]) for h in range(halves)]
+    loads = [pltpu.make_async_copy(w, held.at[i], wsem.at[i]) for i, w in enumerate(sources)]
+    halves_in[0].start()
     barrier = pltpu.get_barrier_semaphore()
     for mask in range(1, peers):
         pl.semaphore_signal(
@@ -161,96 +177,138 @@
                 "space": moved(me_s, steps_s, mask // slots),
             },
         )
-    loads = [pltpu.make_async_copy(w, held.at[i], wsem.at[i]) for i, w in enumerate(sources)]
-    locals_in = [
-        pltpu.make_async_copy(
-            x.at[:, me_t, h], xt.at[h, pl.ds(me_t * rows, rows)], lsem.at[h]
-        )
-        for h in range(halves)
-    ]
-    for copy in locals_in + loads:
+    for copy in halves_in[1:] + loads:
         copy.start()
-    pl.semaphore_wait(barrier, peers - 1)
-
-    def first(h, mask):
+
+    def first(c, mask):
         t = moved(me_t, steps_t, mask)
         return pltpu.make_async_remote_copy(
-            src_ref=x.at[:, t, h],
-            dst_ref=xt.at[h, pl.ds(me_t * rows, rows)],
-            send_sem=s1.at[h, mask],
-            recv_sem=r1.at[h, mask],
+            src_ref=xs.at[c, t],
+            dst_ref=xt.at[c, pl.ds(me_t * rows * few, rows * few)],
+            send_sem=s1.at[c],
+            recv_sem=r1.at[c],
             device_id={"tm": t},
         )
 
-    def second(h, mask, core):
+    def first_all(c):
+        part = xt.at[c, pl.ds(0, (slots - 1) * rows * few)]
+        return pltpu.make_async_remote_copy(
+            src_ref=part,
+            dst_ref=part,
+            send_sem=s1.at[c],
+            recv_sem=r1.at[c],
+            device_id={"tm": moved(me_t, steps_t, 1)},
+        )
+
+    def second(c, mask, core):
         t, z = moved(me_t, steps_t, mask % slots), moved(me_z, steps_z, mask // slots)
         return pltpu.make_async_remote_copy(
-            src_ref=snd.at[h, (t * chips + z) * 2 + core],
-            dst_ref=rcv.at[h * peers + me_s * slots + me_t],
-            send_sem=s2.at[h, mask, core],
-            recv_sem=r2.at[h, mask, me_c],
+            src_ref=snd.at[c, (t * chips + z) * 2 + core],
+            dst_ref=rcv.at[c, me_s * slots + me_t],
+            send_sem=s2.at[c],
+            recv_sem=r2.at[c],
             device_id={"tm": t, "space": z * 2 + core},
         )
 
-    def second_wait(h, mask, core):
+    def second_all(c):
+        part = rcv.at[c, pl.ds(0, peers - 1)]
         return pltpu.make_async_remote_copy(
-            src_ref=snd.at[0, 0],
-            dst_ref=rcv.at[0],
-            send_sem=s2.at[h, mask, core],
-            recv_sem=r2.at[h, mask, core],
-            device_id={"tm": me_t, "space": me_s + 1 - 2 * me_c},
-        )
-
+            src_ref=part,
+            dst_ref=part,
+            send_sem=s2.at[c],
+            recv_sem=r2.at[c],
+            device_id={"space": me_s + 1 - 2 * me_c},
+        )
+
+    def home_row(r):
+        block = rows * few
+        chunk, slot, frame, place = r // (slots * block), (r // block) % slots, (r // few) % rows, r % few
+        return (frame * slots + slot) * piece + chunk * few + place
+
+    per_half = rows * slots * piece
     for h in range(halves):
-        for mask in range(slots - 1, 0, -1):
-            first(h, mask).start()
+        halves_in[h].wait()
+        moved_in = project(one_hot((per_half, per_half), home_row), flat(xv[h])).astype(BF16)
+        for n in range(fold):
+            c = h * fold + n
+            for t in range(slots):
+                start = (n * slots + t) * rows * few
+                xs[c, t] = moved_in[start : start + rows * few]
+            xt[c, pl.ds(me_t * rows * few, rows * few)] = xs[c, me_t]
+        if h == 0:
+            pl.semaphore_wait(barrier, peers - 1)
+        for n in range(fold):
+            for mask in range(slots - 1, 0, -1):
+                first(h * fold + n, mask).start()
 
     weights = [held.at[i] for i in range(8)]
     waits = [copy.wait for copy in loads]
-
-    def send(h, core, masks):
-        for mask in masks:
-            second(h, mask, core).start()
-
-    everyone = list(range(slots * chips - 1, 0, -1))
-    late = []
+    same = (
+        lax.broadcasted_iota(jnp.int32, (size, size), 0) % few
+        == lax.broadcasted_iota(jnp.int32, (size, size), 1) % few
+    )
+    folding = one_hot(
+        (fold * size, fold * size),
+        lambda r: ((r // few) % fold) * size + (r // piece) * few + r % few,
+    )
+    columns = width // fold
+
+    def send(c, core):
+        for mask in range(slots * chips - 1, 0, -1):
+            second(c, mask, core).start()
+
+    for c in range(chunks):
+        first_all(c).wait_recv()
+        part = pl.ds(0, size)
+        tok = xt[c]
+        qkv(
+            layer_norm(tok, tg[...], ts[...]),
+            weights[:3],
+            waits[:3] if c == 0 else [lambda: None] * 3,
+            [ref.at[part] for ref in (q, k, v)],
+        )
+
+        def time_pair(index, carry):
+            cols = pl.ds(pl.multiple_of(index * LANES, LANES), LANES)
+            a[part, cols] = attend(q[part, cols], k[part, cols], v[part, cols], same)
+            return carry
+
+        lax.fori_loop(0, width // LANES, time_pair, 0, unroll=UNROLL_T)
+        if c == 0:
+            waits[3]()
+        after = (tok.astype(F32) + project(a[part], weights[3][...])).astype(BF16)
+        after = jnp.concatenate([after[:, n * columns : (n + 1) * columns] for n in range(fold)], 0)
+        snd[c] = project(folding, after).reshape(frames, piece, columns).astype(BF16)
+        send(c, 0)
+        pltpu.make_async_remote_copy(
+            src_ref=snd.at[c, (me_t * chips + me_z) * 2 + 1 - me_c],
+            dst_ref=rcv.at[c, me_s * slots + me_t],
+            send_sem=s2.at[c],
+            recv_sem=r2.at[c],
+            device_id={"space": me_z * 2 + 1 - me_c},
+        ).start()
+        rcv[c, me_s * slots + me_t] = snd[c, me_t * rows + me_s]
+    for c in range(chunks):
+        send(c, 1)
+
     for h in range(halves):
-        locals_in[h].wait()
-        for mask in range(1, slots):
-            first(h, mask).wait_recv()
-        part = [ref.at[pl.ds(0, tokens)] for ref in (q, k, v, a)]
-        after = time_branch(
-            frames,
-            xt[h].astype(F32).reshape(tokens, width).astype(BF16),
-            tg[...],
-            ts[...],
-            weights[:4],
-            waits[:4] if h == 0 else [lambda: None] * 4,
-            *part,
-        )
-        snd[h] = after.reshape(frames, piece, width).astype(BF16)
-        send(h, 0, everyone)
-        if h < halves - 1:
-            late.append(h)
-        else:
-            for held_back in late + [h]:
-                send(held_back, 1, everyone)
-        other = 1 - me_c
-        pltpu.make_async_remote_copy(
-            src_ref=snd.at[h, (me_t * chips + me_z) * 2 + other],
-            dst_ref=rcv.at[h * peers + me_s * slots + me_t],
-            send_sem=s2.at[h, 0, 0],
-            recv_sem=r2.at[h, 0, 0],
-            device_id={"space": me_z * 2 + other},
-        ).start()
-        rcv[h * peers + me_s * slots + me_t] = snd[h, me_t * rows + me_s]
-
-    for h in range(halves):
-        for mask in everyone:
-            for core in range(2):
-                second_wait(h, mask, core).wait_recv()
-        second_wait(h, 0, 0).wait_recv()
-        frame = rcv[pl.ds(h * peers, peers)].astype(F32).reshape(tokens, width).astype(BF16)
+        for n in range(fold):
+            second_all(h * fold + n).wait_recv()
+        arrived = jnp.concatenate([flat(rcv[h * fold + n]) for n in range(fold)], 0)
+        frame = jnp.concatenate(
+            [
+                project(
+                    one_hot(
+                        (tokens, fold * tokens),
+                        lambda r: ((r // few) % fold) * tokens + (r // piece) * piece + n * few + r % few,
+                    ),
+                    arrived,
+                ).astype(BF16)
+                for n in range(fold)
+            ],
+            1,
+        )
+        res[pl.ds(h * peers, peers)] = frame.astype(F32).reshape(peers, piece, width).astype(BF16)
         qkv(
             layer_norm(frame, sg[...], ss[...]),
             weights[4:7],
@@ -268,7 +326,7 @@
     def third(h, mask):
         s = moved(me_s, steps_s, mask)
         return pltpu.make_async_remote_copy(
-            src_ref=rcv.at[blocks(h, s, 1)],
+            src_ref=res.at[blocks(h, s, 1)],
             dst_ref=out.at[me_s, :, h],
             send_sem=s3.at[h, mask],
             recv_sem=r3.at[h, mask],
@@ -295,26 +353,20 @@
         for h in range(halves):
             here = blocks(h, base, group)
             new = added[h * size : (h + 1) * size].reshape(group * slots, piece, width)
-            rcv[here] = (rcv[here].astype(F32) + new).astype(BF16)
+            res[here] = (res[here].astype(F32) + new).astype(BF16)
         for member in range(group - 1, -1, -1):
             if step * group + member:
                 for h in range(halves):
                     third(h, step * group + member).start()
     last = [
-        pltpu.make_async_copy(rcv.at[blocks(h, me_s, 1)], out.at[me_s, :, h], lsem.at[h])
+        pltpu.make_async_copy(res.at[blocks(h, me_s, 1)], out.at[me_s, :, h], lsem.at[h])
         for h in range(halves)
     ]
     for copy in last:
         copy.start()
-    for h in range(halves):
-        for mask in range(1, slots):
-            first(h, mask).wait_send()
-
-    for h in range(halves):
-        for mask in everyone:
-            for core in range(2):
-                second_wait(h, mask, core).wait_send()
-        second_wait(h, 0, 0).wait_send()
+    for c in range(chunks):
+        first_all(c).wait_send()
+        second_all(c).wait_send()
     for h in range(halves):
         for mask in range(1, spread):
             third(h, mask).wait()
@@ -326,27 +378,33 @@
     frames, places, halves = rows * slots, patches // slots, 2
     piece = places // halves
     total = frames * places
+    few = LANES // frames
+    fold, size = piece // few, frames * few
+    chunks = halves * fold
     vmem, hbm = pl.BlockSpec(memory_space=pltpu.VMEM), pl.BlockSpec(memory_space=pltpu.HBM)
     dma = pltpu.SemaphoreType.DMA
     return pl.pallas_call(
         functools.partial(layer_kernel, slots, spread),
-        out_shape=jax.ShapeDtypeStruct((rows, slots, halves, piece, width), BF16),
+        out_shape=pltpu.VMEM((rows, slots, halves, piece, width), BF16),
         in_specs=[hbm] + [vmem] * 4 + [hbm] * 8,
-        out_specs=hbm,
+        out_specs=vmem,
         scratch_shapes=[
             pltpu.VMEM((8, width, width), BF16),
-            pltpu.VMEM((halves, frames, piece, width), BF16),
-            pltpu.VMEM((halves, frames, piece, width), BF16),
+            pltpu.VMEM((halves, rows, slots, piece, width), BF16),
+            pltpu.VMEM((chunks, slots, rows * few, width), BF16),
+            pltpu.VMEM((chunks, size, width), BF16),
+            pltpu.VMEM((chunks, frames, piece, width // fold), BF16),
+            pltpu.VMEM((chunks, slots * spread, piece, width // fold), BF16),
             pltpu.VMEM((total // piece, piece, width), BF16),
         ]
         + [pltpu.VMEM((total, width), BF16)] * 4
         + [
             dma((8,)),
             dma((halves,)),
-            dma((halves, slots)),
-            dma((halves, slots)),
-            dma((halves, slots * spread // 2, 2)),
-            dma((halves, slots * spread // 2, 2)),
+            dma((chunks,)),
+            dma((chunks,)),
+            dma((chunks,)),
+            dma((chunks,)),
             dma((halves, spread)),
             dma((halves, spread)),
         ],
@@ -384,7 +442,9 @@
     slots, spread = lax.axis_size("tm"), lax.axis_size("space")
     rows, patches, width = frames_in.shape
     frames, places = rows * slots, patches // slots
-    if rows == spread and spread % 2 == 0 and not (slots & (slots - 1) or spread & (spread - 1)):
+    powers = not (slots & (slots - 1) or spread & (spread - 1)) and spread % 2 == 0
+    tiles = places == 16 and LANES % frames == 0 and LANES // frames in (2, 4, 8)
+    if rows == spread and powers and tiles:
         return run_layer(
             frames_in, slots, spread, (tg, ts, sg, ss), (tq, tk, tv, to, sq, sk, sv, so)
         )

time: 71.6 us -> 65.8 us (0.919)
  Pallas kernels: 68.3 us -> 63.9 us
  local copies, waits for them, and re-layouts: 2.26 us -> 0.97 us
    pallas_call x1, Pallas kernels: 68.3 us -> 63.9 us  [run_layer(): pl.pallas_call(functools.partial(layer_kernel, slots, spread), out_shape=...]
    unnamed x1, local copies, waits for them, and re-layouts: 2.26 us -> 0.97 us
where the time goes in v2:
time: 65.8 us; the launch traced here: 64.8 us
  Pallas kernels  63.9 us (97%)
  local copies, waits for them, and re-layouts  0.97 us (1%)
    pallas_call x1, Pallas kernels, run_layer(): pl.pallas_call(functools.partial(layer_kernel, slots, spread), out_shape=...  63.9 us

profile of v2, /device:TPU:0, one launch (start us, length us, event | category | flops | bytes accessed | tf_op | source)
XLA Modules:
  0.0 64.8 jit_solution(453139140258496352)
XLA Ops:
  0.0 63.9 %shard_map.127 = bf16[8,4,2,8,1024]{4,3,2,1,0:T(8,128)(2,1)S(1)} custom-call(bf16[8,4,2,8,1024]{4,3,2,1,0:T(8,128)(2,1)} %bitcast.7, f32[1,1024]{1,0:T(1,128)} %bitcast.8, f32[1,1024]{1,0:T(1,128)} %bitcast.9, f32[1,1024]{1,0:T(1,128)} %bitcast.10, f32[1,1024]{1,0:T(1,128)} %bitcast.11, bf16[1024,1024]{1,0:T(8,128)(2,1)} %refs_0_.1, ...), custom_call_target="tpu_custom_call" | custom-call | tf_op jit(solution)/shard_map/pallas_call | solution.py:386
  63.9 1.0 %copy.15 = bf16[8,64,1024]{2,1,0:T(8,128)(2,1)} copy(bf16[8,64,1024]{2,1,0:T(8,128)(2,1)S(1)} %bitcast.6) | data formatting | bytes 2097152

commit v3 on v2

--- a/solution.py
+++ b/solution.py
@@ -142,14 +142,10 @@
     slots,
     spread,
     x,
-    tg,
-    ts,
-    sg,
-    ss,
     *refs,
 ):
-    sources, out = refs[:8], refs[8]
-    held, xv, xs, xt, snd, rcv, res, q, k, v, a, wsem, lsem, s1, r1, s2, r2, s3, r3 = refs[9:]
+    scales, sources, out = refs[:4], refs[4:12], refs[12]
+    norms, held, xv, xs, xt, snd, rcv, res, q, k, v, a, nsem, wsem, lsem, s1, r1, s2, r2, s3, r3 = refs[13:]
     me_t, me_s = lax.axis_index("tm"), lax.axis_index("space")
     halves, rows, _, piece, width = xv.shape
     chunks, size, _ = xt.shape
@@ -166,6 +162,7 @@
 
     halves_in = [pltpu.make_async_copy(x.at[:, :, h], xv.at[h], lsem.at[h]) for h in range(halves)]
     loads = [pltpu.make_async_copy(w, held.at[i], wsem.at[i]) for i, w in enumerate(sources)]
+    norms_in = [pltpu.make_async_copy(n, norms.at[i], nsem.at[i]) for i, n in enumerate(scales)]
     halves_in[0].start()
     barrier = pltpu.get_barrier_semaphore()
     for mask in range(1, peers):
@@ -177,7 +174,7 @@
                 "space": moved(me_s, steps_s, mask // slots),
             },
         )
-    for copy in halves_in[1:] + loads:
+    for copy in halves_in[1:] + norms_in + loads:
         copy.start()
 
     def first(c, mask):
@@ -243,6 +240,9 @@
 
     weights = [held.at[i] for i in range(8)]
     waits = [copy.wait for copy in loads]
+    for copy in norms_in:
+        copy.wait()
+    tg, ts, sg, ss = [norms.at[i] for i in range(4)]
     same = (
         lax.broadcasted_iota(jnp.int32, (size, size), 0) % few
         == lax.broadcasted_iota(jnp.int32, (size, size), 1) % few
@@ -308,7 +308,7 @@
             ],
             1,
         )
-        res[pl.ds(h * peers, peers)] = frame.astype(F32).reshape(peers, piece, width).astype(BF16)
+        res[:, :, h] = frame.astype(F32).reshape(spread, slots, piece, width).astype(BF16)
         qkv(
             layer_norm(frame, sg[...], ss[...]),
             weights[4:7],
@@ -317,27 +317,23 @@
         )
     waits[7]()
     share = slots * piece
-    group = 2 if spread % 2 == 0 else 1
-    steps = spread // group
-
-    def blocks(h, s, count):
-        return pl.ds(h * peers + s * slots, count * slots)
-
-    def third(h, mask):
-        s = moved(me_s, steps_s, mask)
+    both = 2 * share
+
+    def third(target):
         return pltpu.make_async_remote_copy(
-            src_ref=res.at[blocks(h, s, 1)],
-            dst_ref=out.at[me_s, :, h],
-            send_sem=s3.at[h, mask],
-            recv_sem=r3.at[h, mask],
-            device_id={"space": s},
-        )
-
-    for step in range(steps - 1, -1, -1):
-        size = group * share
-        base = moved(me_s // group, bit_steps(me_s // group, steps), step) * group
+            src_ref=res.at[target],
+            dst_ref=out.at[me_s],
+            send_sem=s3,
+            recv_sem=r3,
+            device_id={"space": target},
+        )
+
+    near = chips // 2
+    targets = [(1 - me_z // near) * near + n for n in range(near)] if near else []
+    targets += [moved(me_z, steps_z, mask) for mask in range(near - 1, 0, -1)]
+    for target in targets + [me_z]:
         parts = [
-            pl.ds(pl.multiple_of(h * tokens + base * share, size), size) for h in range(halves)
+            pl.ds(pl.multiple_of(h * tokens + target * both, both), both) for h in range(halves)
         ]
 
         def attend_pair(index, carry):
@@ -345,32 +341,34 @@
             queries = jnp.concatenate([q[part, cols] for part in parts], 0)
             result = attend(queries, k[:, cols], v[:, cols], None)
             for h, part in enumerate(parts):
-                a[part, cols] = result[h * size : (h + 1) * size]
+                a[part, cols] = result[h * both : (h + 1) * both]
             return carry
 
         lax.fori_loop(0, width // LANES, attend_pair, 0, unroll=UNROLL_S)
         added = project(jnp.concatenate([a[part] for part in parts], 0), weights[7][...])
+        here = pl.ds(2 * target, 2)
         for h in range(halves):
-            here = blocks(h, base, group)
-            new = added[h * size : (h + 1) * size].reshape(group * slots, piece, width)
-            res[here] = (res[here].astype(F32) + new).astype(BF16)
-        for member in range(group - 1, -1, -1):
-            if step * group + member:
-                for h in range(halves):
-                    third(h, step * group + member).start()
-    last = [
-        pltpu.make_async_copy(res.at[blocks(h, me_s, 1)], out.at[me_s, :, h], lsem.at[h])
-        for h in range(halves)
-    ]
-    for copy in last:
-        copy.start()
+            new = added[h * both : (h + 1) * both].reshape(2, slots, piece, width)
+            res[here, :, h] = (res[here, :, h].astype(F32) + new).astype(BF16)
+        if target is me_z:
+            third(me_s + 1 - 2 * me_c).start()
+        else:
+            for core in range(2):
+                third(2 * target + core).start()
+    last = pltpu.make_async_copy(res.at[me_s], out.at[me_s], lsem.at[0])
+    last.start()
     for c in range(chunks):
         first_all(c).wait_send()
         second_all(c).wait_send()
-    for h in range(halves):
-        for mask in range(1, spread):
-            third(h, mask).wait()
-        last[h].wait()
+    others = pl.ds(0, spread - 1)
+    pltpu.make_async_remote_copy(
+        src_ref=res.at[others],
+        dst_ref=out.at[others],
+        send_sem=s3,
+        recv_sem=r3,
+        device_id={"space": me_s + 1 - 2 * me_c},
+    ).wait()
+    last.wait()
 
 
 def run_layer(frames_in, slots, spread, norms, weights):
@@ -386,27 +384,29 @@
     return pl.pallas_call(
         functools.partial(layer_kernel, slots, spread),
         out_shape=pltpu.VMEM((rows, slots, halves, piece, width), BF16),
-        in_specs=[hbm] + [vmem] * 4 + [hbm] * 8,
+        in_specs=[hbm] * 13,
         out_specs=vmem,
         scratch_shapes=[
+            pltpu.VMEM((4, 1, width), F32),
             pltpu.VMEM((8, width, width), BF16),
             pltpu.VMEM((halves, rows, slots, piece, width), BF16),
             pltpu.VMEM((chunks, slots, rows * few, width), BF16),
             pltpu.VMEM((chunks, size, width), BF16),
             pltpu.VMEM((chunks, frames, piece, width // fold), BF16),
             pltpu.VMEM((chunks, slots * spread, piece, width // fold), BF16),
-            pltpu.VMEM((total // piece, piece, width), BF16),
+            pltpu.VMEM((spread, slots, halves, piece, width), BF16),
         ]
         + [pltpu.VMEM((total, width), BF16)] * 4
         + [
+            dma((4,)),
             dma((8,)),
             dma((halves,)),
             dma((chunks,)),
             dma((chunks,)),
             dma((chunks,)),
             dma((chunks,)),
-            dma((halves, spread)),
-            dma((halves, spread)),
+            dma(()),
+            dma(()),
         ],
         compiler_params=pltpu.CompilerParams(
             collective_id=0, has_side_effects=True, vmem_limit_bytes=60 << 20

time: 65.8 us -> 63.9 us (0.971)
  the two profiles are of different devices: /device:TPU:0 before, /device:TPU:29 now
where the time goes in v3:
time: 63.9 us; the launch traced here: 63.8 us
  Pallas kernels  62.8 us (98%)
  local copies, waits for them, and re-layouts  0.97 us (2%)
    pallas_call x1, Pallas kernels, run_layer(): pl.pallas_call(functools.partial(layer_kernel, slots, spread), out_shape=...  62.8 us

profile of v3, /device:TPU:29, one launch (start us, length us, event | category | flops | bytes accessed | tf_op | source)
XLA Modules:
  0.0 63.8 jit_solution(4840404388455005051)
XLA Ops:
  0.0 62.8 %shard_map.127 = bf16[8,4,2,8,1024]{4,3,2,1,0:T(8,128)(2,1)S(1)} custom-call(bf16[8,4,2,8,1024]{4,3,2,1,0:T(8,128)(2,1)} %bitcast.7, f32[1,1024]{1,0:T(1,128)} %bitcast.8, f32[1,1024]{1,0:T(1,128)} %bitcast.9, f32[1,1024]{1,0:T(1,128)} %bitcast.10, f32[1,1024]{1,0:T(1,128)} %bitcast.11, bf16[1024,1024]{1,0:T(8,128)(2,1)} %refs_4_.1, ...), custom_call_target="tpu_custom_call" | custom-call | tf_op jit(solution)/shard_map/pallas_call | solution.py:384
  62.8 1.0 %copy.15 = bf16[8,64,1024]{2,1,0:T(8,128)(2,1)} copy(bf16[8,64,1024]{2,1,0:T(8,128)(2,1)S(1)} %bitcast.6) | data formatting | bytes 2097152

commit v4 on v3

--- a/solution.py
+++ b/solution.py
@@ -11,6 +11,8 @@
 HEAD_DIM = 64
 LANES = 128
 UNROLL_T, UNROLL_S = 8, 8
+PLAN = ((4, 4), (4, 4))
+EARLY = (3, 3, 0, 0)
 SCALE = 0.125 * math.log2(math.e)
 F32, BF16 = jnp.float32, jnp.bfloat16
 
@@ -129,7 +131,7 @@
 
 
 def one_hot(shape, source):
-    row = lax.broadcasted_iota(jnp.int32, shape, 0)
+    row = lax.broadcasted_iota(jnp.int32, (shape[0], 1), 0)
     col = lax.broadcasted_iota(jnp.int32, shape, 1)
     return jnp.where(source(row) == col, 1.0, 0.0).astype(BF16)
 
@@ -145,13 +147,13 @@
     *refs,
 ):
     scales, sources, out = refs[:4], refs[4:12], refs[12]
-    norms, held, xv, xs, xt, snd, rcv, res, q, k, v, a, nsem, wsem, lsem, s1, r1, s2, r2, s3, r3 = refs[13:]
+    norms, held, xv, res, q, k, v, a, nsem, wsem, lsem, s1, r1, s2, r2, s3, r3 = refs[13:30]
+    chunks = [(h, sum(plan[:n]), few) for h, plan in enumerate(PLAN) for n, few in enumerate(plan)]
+    count = len(chunks)
+    xs, xt, snd, rcv = [refs[30 + n * count : 30 + (n + 1) * count] for n in range(4)]
     me_t, me_s = lax.axis_index("tm"), lax.axis_index("space")
     halves, rows, _, piece, width = xv.shape
-    chunks, size, _ = xt.shape
     frames = rows * slots
-    few = size // frames
-    fold = piece // few
     peers = slots * spread
     chips = spread // 2
     tokens = frames * piece
@@ -180,15 +182,15 @@
     def first(c, mask):
         t = moved(me_t, steps_t, mask)
         return pltpu.make_async_remote_copy(
-            src_ref=xs.at[c, t],
-            dst_ref=xt.at[c, pl.ds(me_t * rows * few, rows * few)],
+            src_ref=xs[c].at[t],
+            dst_ref=xt[c].at[pl.ds(me_t * rows * chunks[c][2], rows * chunks[c][2])],
             send_sem=s1.at[c],
             recv_sem=r1.at[c],
             device_id={"tm": t},
         )
 
     def first_all(c):
-        part = xt.at[c, pl.ds(0, (slots - 1) * rows * few)]
+        part = xt[c].at[pl.ds(0, (slots - 1) * rows * chunks[c][2])]
         return pltpu.make_async_remote_copy(
             src_ref=part,
             dst_ref=part,
@@ -200,15 +202,15 @@
     def second(c, mask, core):
         t, z = moved(me_t, steps_t, mask % slots), moved(me_z, steps_z, mask // slots)
         return pltpu.make_async_remote_copy(
-            src_ref=snd.at[c, (t * chips + z) * 2 + core],
-            dst_ref=rcv.at[c, me_s * slots + me_t],
+            src_ref=snd[c].at[(t * chips + z) * 2 + core],
+            dst_ref=rcv[c].at[me_s * slots + me_t],
             send_sem=s2.at[c],
             recv_sem=r2.at[c],
             device_id={"tm": t, "space": z * 2 + core},
         )
 
     def second_all(c):
-        part = rcv.at[c, pl.ds(0, peers - 1)]
+        part = rcv[c].at[pl.ds(0, peers - 1)]
         return pltpu.make_async_remote_copy(
             src_ref=part,
             dst_ref=part,
@@ -217,50 +219,65 @@
             device_id={"space": me_s + 1 - 2 * me_c},
         )
 
-    def home_row(r):
-        block = rows * few
-        chunk, slot, frame, place = r // (slots * block), (r // block) % slots, (r // few) % rows, r % few
-        return (frame * slots + slot) * piece + chunk * few + place
-
-    per_half = rows * slots * piece
+    def home(h):
+        def source(r):
+            found = r
+            for own, first_place, few in chunks:
+                if own == h:
+                    start, block = first_place * slots * rows, rows * few
+                    n = r - start
+                    place = first_place + n % few
+                    row = (((n // few) % rows) * slots + (n // block) % slots) * piece + place
+                    found = jnp.where(r >= start, row, found)
+            return found
+
+        return one_hot((rows * slots * piece,) * 2, source)
+
+    same, folding = {}, {}
+    first_home = home(0)
+    for few in sorted({few for _, _, few in chunks}):
+        size, fold = frames * few, piece // few
+        same[few] = (
+            lax.broadcasted_iota(jnp.int32, (size, 1), 0) % few
+            == lax.broadcasted_iota(jnp.int32, (1, size), 1) % few
+        )
+        folding[few] = one_hot(
+            (fold * size,) * 2,
+            lambda r: ((r // few) % fold) * size + (r // piece) * few + r % few,
+        )
+
     for h in range(halves):
         halves_in[h].wait()
-        moved_in = project(one_hot((per_half, per_half), home_row), flat(xv[h])).astype(BF16)
-        for n in range(fold):
-            c = h * fold + n
-            for t in range(slots):
-                start = (n * slots + t) * rows * few
-                xs[c, t] = moved_in[start : start + rows * few]
-            xt[c, pl.ds(me_t * rows * few, rows * few)] = xs[c, me_t]
+        moved_in = project(first_home if h == 0 else home(h), flat(xv[h])).astype(BF16)
+        for c, (own, first_place, few) in enumerate(chunks):
+            if own == h:
+                block = rows * few
+                for t in range(slots):
+                    start = first_place * slots * rows + t * block
+                    xs[c][t] = moved_in[start : start + block]
+                xt[c][pl.ds(me_t * block, block)] = xs[c][me_t]
         if h == 0:
             pl.semaphore_wait(barrier, peers - 1)
-        for n in range(fold):
-            for mask in range(slots - 1, 0, -1):
-                first(h * fold + n, mask).start()
+        for c, (own, _, _) in enumerate(chunks):
+            if own == h:
+                for mask in range(slots - 1, 0, -1):
+                    first(c, mask).start()
 
     weights = [held.at[i] for i in range(8)]
     waits = [copy.wait for copy in loads]
     for copy in norms_in:
         copy.wait()
     tg, ts, sg, ss = [norms.at[i] for i in range(4)]
-    same = (
-        lax.broadcasted_iota(jnp.int32, (size, size), 0) % few
-        == lax.broadcasted_iota(jnp.int32, (size, size), 1) % few
-    )
-    folding = one_hot(
-        (fold * size, fold * size),
-        lambda r: ((r // few) % fold) * size + (r // piece) * few + r % few,
-    )
-    columns = width // fold
-
-    def send(c, core):
-        for mask in range(slots * chips - 1, 0, -1):
+    def send(c, core, masks):
+        for mask in masks:
             second(c, mask, core).start()
 
-    for c in range(chunks):
+    everyone = list(range(slots * chips - 1, 0, -1))
+    for c, (_, _, few) in enumerate(chunks):
         first_all(c).wait_recv()
-        part = pl.ds(0, size)
-        tok = xt[c]
+        size, fold = frames * few, piece // few
+        part, columns = pl.ds(0, size), width // fold
+        tok = xt[c][...]
         qkv(
             layer_norm(tok, tg[...], ts[...]),
             weights[:3],
@@ -270,7 +287,7 @@
 
         def time_pair(index, carry):
             cols = pl.ds(pl.multiple_of(index * LANES, LANES), LANES)
-            a[part, cols] = attend(q[part, cols], k[part, cols], v[part, cols], same)
+            a[part, cols] = attend(q[part, cols], k[part, cols], v[part, cols], same[few])
             return carry
 
         lax.fori_loop(0, width // LANES, time_pair, 0, unroll=UNROLL_T)
@@ -278,36 +295,46 @@
             waits[3]()
         after = (tok.astype(F32) + project(a[part], weights[3][...])).astype(BF16)
         after = jnp.concatenate([after[:, n * columns : (n + 1) * columns] for n in range(fold)], 0)
-        snd[c] = project(folding, after).reshape(frames, piece, columns).astype(BF16)
-        send(c, 0)
+        if fold > 1:
+            after = project(folding[few], after)
+        snd[c][...] = after.astype(F32).reshape(frames, piece, columns).astype(BF16)
+        send(c, 0, everyone)
         pltpu.make_async_remote_copy(
-            src_ref=snd.at[c, (me_t * chips + me_z) * 2 + 1 - me_c],
-            dst_ref=rcv.at[c, me_s * slots + me_t],
+            src_ref=snd[c].at[(me_t * chips + me_z) * 2 + 1 - me_c],
+            dst_ref=rcv[c].at[me_s * slots + me_t],
             send_sem=s2.at[c],
             recv_sem=r2.at[c],
             device_id={"space": me_z * 2 + 1 - me_c},
         ).start()
-        rcv[c, me_s * slots + me_t] = snd[c, me_t * rows + me_s]
-    for c in range(chunks):
-        send(c, 1)
+        send(c, 1, everyone[: EARLY[c]])
+        rcv[c][me_s * slots + me_t] = snd[c][me_t * rows + me_s]
+    for c in range(count):
+        send(c, 1, everyone[EARLY[c] :])
 
     for h in range(halves):
-        for n in range(fold):
-            second_all(h * fold + n).wait_recv()
-        arrived = jnp.concatenate([flat(rcv[h * fold + n]) for n in range(fold)], 0)
-        frame = jnp.concatenate(
-            [
-                project(
-                    one_hot(
-                        (tokens, fold * tokens),
-                        lambda r: ((r // few) % fold) * tokens + (r // piece) * piece + n * few + r % few,
-                    ),
-                    arrived,
-                ).astype(BF16)
-                for n in range(fold)
-            ],
-            1,
-        )
+        mine = [(c, first_place, few) for c, (own, first_place, few) in enumerate(chunks) if own == h]
+        for c, _, _ in mine:
+            second_all(c).wait_recv()
+        arrived = [(flat(rcv[c][...]), first_place, few) for c, first_place, few in mine]
+        finest = max(piece // few for _, _, few in arrived)
+        columns = width // finest
+        parts = []
+        for n in range(finest):
+            def source(r):
+                place, found = r % piece, r
+                for m, (_, first_place, few) in enumerate(arrived):
+                    part = n * piece // (finest * few)
+                    row = m * tokens + (r // piece) * piece + part * few + place - first_place
+                    found = jnp.where(place >= first_place, row, found)
+                return found
+
+            stack = []
+            for block, _, few in arrived:
+                start = (n % (finest * few // piece)) * columns
+                stack.append(block[:, start : start + columns])
+            hot = one_hot((tokens, len(arrived) * tokens), source)
+            parts.append(project(hot, jnp.concatenate(stack, 0)).astype(BF16))
+        frame = jnp.concatenate(parts, 1)
         res[:, :, h] = frame.astype(F32).reshape(spread, slots, piece, width).astype(BF16)
         qkv(
             layer_norm(frame, sg[...], ss[...]),
@@ -353,11 +380,11 @@
         if target is me_z:
             third(me_s + 1 - 2 * me_c).start()
         else:
-            for core in range(2):
+            for core in (1, 0):
                 third(2 * target + core).start()
     last = pltpu.make_async_copy(res.at[me_s], out.at[me_s], lsem.at[0])
     last.start()
-    for c in range(chunks):
+    for c in range(count):
         first_all(c).wait_send()
         second_all(c).wait_send()
     others = pl.ds(0, spread - 1)
@@ -376,9 +403,7 @@
     frames, places, halves = rows * slots, patches // slots, 2
     piece = places // halves
     total = frames * places
-    few = LANES // frames
-    fold, size = piece // few, frames * few
-    chunks = halves * fold
+    fews = [few for plan in PLAN for few in plan]
     vmem, hbm = pl.BlockSpec(memory_space=pltpu.VMEM), pl.BlockSpec(memory_space=pltpu.HBM)
     dma = pltpu.SemaphoreType.DMA
     return pl.pallas_call(
@@ -390,10 +415,6 @@
             pltpu.VMEM((4, 1, width), F32),
             pltpu.VMEM((8, width, width), BF16),
             pltpu.VMEM((halves, rows, slots, piece, width), BF16),
-            pltpu.VMEM((chunks, slots, rows * few, width), BF16),
-            pltpu.VMEM((chunks, size, width), BF16),
-            pltpu.VMEM((chunks, frames, piece, width // fold), BF16),
-            pltpu.VMEM((chunks, slots * spread, piece, width // fold), BF16),
             pltpu.VMEM((spread, slots, halves, piece, width), BF16),
         ]
         + [pltpu.VMEM((total, width), BF16)] * 4
@@ -401,13 +422,17 @@
             dma((4,)),
             dma((8,)),
             dma((halves,)),
-            dma((chunks,)),
-            dma((chunks,)),
-            dma((chunks,)),
-            dma((chunks,)),
+            dma((len(fews),)),
+            dma((len(fews),)),
+            dma((len(fews),)),
+            dma((len(fews),)),
             dma(()),
             dma(()),
-        ],
+        ]
+        + [pltpu.VMEM((slots, rows * few, width), BF16) for few in fews]
+        + [pltpu.VMEM((frames * few, width), BF16) for few in fews]
+        + [pltpu.VMEM((frames, piece, width * few // piece), BF16) for few in fews]
+        + [pltpu.VMEM((slots * spread, piece, width * few // piece), BF16) for few in fews],
         compiler_params=pltpu.CompilerParams(
             collective_id=0, has_side_effects=True, vmem_limit_bytes=60 << 20
         ),
@@ -443,7 +468,7 @@
     rows, patches, width = frames_in.shape
     frames, places = rows * slots, patches // slots
     powers = not (slots & (slots - 1) or spread & (spread - 1)) and spread % 2 == 0
-    tiles = places == 16 and LANES % frames == 0 and LANES // frames in (2, 4, 8)
+    tiles = places == 16 and width % (4 * LANES) == 0
     if rows == spread and powers and tiles:
         return run_layer(
             frames_in, slots, spread, (tg, ts, sg, ss), (tq, tk, tv, to, sq, sk, sv, so)

time: 63.9 us -> 61.2 us (0.958)
  the two profiles are of different devices: /device:TPU:29 before, /device:TPU:28 now
where the time goes in v4:
time: 61.2 us; the launch traced here: 61.1 us
  Pallas kernels  60.1 us (98%)
  local copies, waits for them, and re-layouts  0.97 us (2%)
    pallas_call x1, Pallas kernels, run_layer(): pl.pallas_call(functools.partial(layer_kernel, slots, spread), out_shape=...  60.1 us

profile of v4, /device:TPU:28, one launch (start us, length us, event | category | flops | bytes accessed | tf_op | source)
XLA Modules:
  0.0 61.1 jit_solution(471892365127278480)
XLA Ops:
  0.0 60.1 %shard_map.127 = bf16[8,4,2,8,1024]{4,3,2,1,0:T(8,128)(2,1)S(1)} custom-call(bf16[8,4,2,8,1024]{4,3,2,1,0:T(8,128)(2,1)} %bitcast.7, f32[1,1024]{1,0:T(1,128)} %bitcast.8, f32[1,1024]{1,0:T(1,128)} %bitcast.9, f32[1,1024]{1,0:T(1,128)} %bitcast.10, f32[1,1024]{1,0:T(1,128)} %bitcast.11, bf16[1024,1024]{1,0:T(8,128)(2,1)} %refs_4_.1, ...), custom_call_target="tpu_custom_call" | custom-call | tf_op jit(solution)/shard_map/pallas_call | solution.py:409
  60.1 1.0 %copy.15 = bf16[8,64,1024]{2,1,0:T(8,128)(2,1)} copy(bf16[8,64,1024]{2,1,0:T(8,128)(2,1)S(1)} %bitcast.6) | data formatting | bytes 2097152

commit v5 on v4

--- a/solution.py
+++ b/solution.py
@@ -11,8 +11,8 @@
 HEAD_DIM = 64
 LANES = 128
 UNROLL_T, UNROLL_S = 8, 8
-PLAN = ((4, 4), (4, 4))
-EARLY = (3, 3, 0, 0)
+PLAN = ((2, 2, 4), (4, 4))
+EARLY = (7, 7, 2, 0, 0)
 SCALE = 0.125 * math.log2(math.e)
 F32, BF16 = jnp.float32, jnp.bfloat16
 

time: 61.2 us -> 60.1 us (0.982)
  the two profiles are of different devices: /device:TPU:28 before, /device:TPU:8 now
where the time goes in v5:
time: 60.1 us; the launch traced here: 60 us
  Pallas kernels  59 us (98%)
  local copies, waits for them, and re-layouts  0.97 us (2%)
    pallas_call x1, Pallas kernels, run_layer(): pl.pallas_call(functools.partial(layer_kernel, slots, spread), out_shape=...  59 us

profile of v5, /device:TPU:8, one launch (start us, length us, event | category | flops | bytes accessed | tf_op | source)
XLA Modules:
  0.0 60.0 jit_solution(59174053763223431)
XLA Ops:
  0.0 59.0 %shard_map.127 = bf16[8,4,2,8,1024]{4,3,2,1,0:T(8,128)(2,1)S(1)} custom-call(bf16[8,4,2,8,1024]{4,3,2,1,0:T(8,128)(2,1)} %bitcast.7, f32[1,1024]{1,0:T(1,128)} %bitcast.8, f32[1,1024]{1,0:T(1,128)} %bitcast.9, f32[1,1024]{1,0:T(1,128)} %bitcast.10, f32[1,1024]{1,0:T(1,128)} %bitcast.11, bf16[1024,1024]{1,0:T(8,128)(2,1)} %refs_4_.1, ...), custom_call_target="tpu_custom_call" | custom-call | tf_op jit(solution)/shard_map/pallas_call | solution.py:409
  59.0 1.0 %copy.15 = bf16[8,64,1024]{2,1,0:T(8,128)(2,1)} copy(bf16[8,64,1024]{2,1,0:T(8,128)(2,1)S(1)} %bitcast.6) | data formatting | bytes 2097152

commit v6 on v5

--- a/solution.py
+++ b/solution.py
@@ -273,6 +273,7 @@
             second(c, mask, core).start()
 
     everyone = list(range(slots * chips - 1, 0, -1))
+    straight = sorted(everyone, key=lambda mask: mask % slots > 0)
     for c, (_, _, few) in enumerate(chunks):
         first_all(c).wait_recv()
         size, fold = frames * few, piece // few
@@ -298,7 +299,7 @@
         if fold > 1:
             after = project(folding[few], after)
         snd[c][...] = after.astype(F32).reshape(frames, piece, columns).astype(BF16)
-        send(c, 0, everyone)
+        send(c, 0, straight)
         pltpu.make_async_remote_copy(
             src_ref=snd[c].at[(me_t * chips + me_z) * 2 + 1 - me_c],
             dst_ref=rcv[c].at[me_s * slots + me_t],

time: 60.1 us -> 60.5 us (level)
  no operation moved by 1% of the time
where the time goes in v6:
time: 60.5 us; the launch traced here: 60.4 us
  Pallas kernels  59.4 us (98%)
  local copies, waits for them, and re-layouts  0.97 us (2%)
    pallas_call x1, Pallas kernels, run_layer(): pl.pallas_call(functools.partial(layer_kernel, slots, spread), out_shape=...  59.4 us

profile of v6, /device:TPU:8, one launch (start us, length us, event | category | flops | bytes accessed | tf_op | source)
XLA Modules:
  0.0 60.4 jit_solution(2930266174848839935)
XLA Ops:
  0.0 59.4 %shard_map.127 = bf16[8,4,2,8,1024]{4,3,2,1,0:T(8,128)(2,1)S(1)} custom-call(bf16[8,4,2,8,1024]{4,3,2,1,0:T(8,128)(2,1)} %bitcast.7, f32[1,1024]{1,0:T(1,128)} %bitcast.8, f32[1,1024]{1,0:T(1,128)} %bitcast.9, f32[1,1024]{1,0:T(1,128)} %bitcast.10, f32[1,1024]{1,0:T(1,128)} %bitcast.11, bf16[1024,1024]{1,0:T(8,128)(2,1)} %refs_4_.1, ...), custom_call_target="tpu_custom_call" | custom-call | tf_op jit(solution)/shard_map/pallas_call | solution.py:410
  59.4 1.0 %copy.15 = bf16[8,64,1024]{2,1,0:T(8,128)(2,1)} copy(bf16[8,64,1024]{2,1,0:T(8,128)(2,1)S(1)} %bitcast.6) | data formatting | bytes 2097152
